TPU v7x, 32 devices: a whole 2x2x4 slice. The times are simulated.
32 devices in a mesh: dom: 8 (over z, x), attr: 4 (over y, core).
Axes of the slice: x: 2, y: 2, z: 4, core: 2. Of those that a mesh axis runs over, the one named last changes fastest.
Arguments:
- records: bfloat16 [12288, 1024], P('dom', 'attr'), may hold values from -6 to 6
- owner: int32 [12288, 1], P('dom'), may hold values from 0 to 7; in each aligned block of 1536 rows (0 to 1535, 1536 to 3071, ...) at most 384 rows name the same one
- entity_means: bfloat16 [4096, 1024], P('dom', 'attr'), may hold values from -6 to 6
- noise_bits: int32 [24576, 512], P('dom'), may hold values from 0 to 8191
Outputs:
- new_means: float32 [4096, 1024], P('dom', 'attr')
- gram: float32 [1024, 1024], P(('dom', 'attr'))
Inputs may be any that keep to these rules, and one draw needn't show every extreme that they name: `owner`: among the records of one index of dom at most 384 name the same partition, and in every draw some partition is named by exactly 384 of them.
All inputs are finite; a program needn't handle non-finite values.
Results may differ from a plain program's by a relative error of at most 0.0013.
Values may be sent and summed in bfloat16 or wider, within the bound.
A program may use at most 64 MiB of HBM per device.

v0:
```python
import jax
import jax.numpy as jnp
from jax import lax
from jax.sharding import PartitionSpec as P


def posterior(raw, bits, live, width):
    uniform = (bits.astype(jnp.float32) + 0.5) / 8192.0
    noise = -jnp.log(-jnp.log(uniform))
    logits = 3.0 * jnp.tanh(raw * width ** (-0.5)) + noise
    expd = jnp.exp(logits)
    return (expd / jnp.sum(expd, axis=1, keepdims=True) * live[:, None]).astype(jnp.bfloat16)


def shards(records, owner, entity_means, noise_bits):
    dom_count = lax.axis_size("dom")
    attr_count = lax.axis_size("attr")
    rec_dev, feat_cols = records.shape
    slot_count = 2 * rec_dev
    capacity = slot_count // dom_count
    width = feat_cols * attr_count
    total_records = rec_dev * dom_count
    dest = owner[:, 0]
    onehot = (dest[:, None] == jnp.arange(dom_count, dtype=jnp.int32)[None, :]).astype(jnp.int32)
    rank = jnp.sum(jnp.cumsum(onehot, axis=0) * onehot, axis=1) - 1
    position = dest * capacity + rank
    packed = jnp.zeros((slot_count, feat_cols), jnp.bfloat16).at[position].set(records)
    flag_buf = (
        jnp.zeros((slot_count,), jnp.bfloat16).at[position].set(jnp.ones((rec_dev,), jnp.bfloat16))
    )
    arrived, arrived_flags = (
        lax.all_to_all(
            packed.reshape(dom_count, capacity, feat_cols),
            "dom",
            split_axis=0,
            concat_axis=0,
            tiled=True,
        ),
        lax.all_to_all(
            flag_buf.reshape(dom_count, capacity), "dom", split_axis=0, concat_axis=0, tiled=True
        ),
    )
    arrived = arrived.reshape(slot_count, feat_cols)
    live = arrived_flags.reshape(slot_count).astype(jnp.float32)
    raw = lax.psum(jnp.dot(arrived, entity_means.T, preferred_element_type=jnp.float32), "attr")
    weights = posterior(raw, noise_bits, live, width)
    sums_cols = jnp.dot(weights.T, arrived, preferred_element_type=jnp.float32)
    mass_col = jnp.sum(weights.astype(jnp.float32), axis=0)[:, None]
    recon = jnp.dot(weights, entity_means, preferred_element_type=jnp.float32)
    col_resid = ((arrived.astype(jnp.float32) - recon) * live[:, None]).astype(jnp.bfloat16)
    residual = lax.all_to_all(col_resid, "attr", split_axis=0, concat_axis=1, tiled=True)
    new_means = (sums_cols + 1.0 * entity_means.astype(jnp.float32)) / (mass_col + 1.0)
    term = lax.dot_general(
        residual, residual, (((0,), (0,)), ((), ())), preferred_element_type=jnp.float32
    )
    gram = lax.psum_scatter(term / total_records, ("dom", "attr"), scatter_dimension=0, tiled=True)
    return (new_means, gram)


def solution(mesh):
    in_specs = (P("dom", "attr"), P("dom", None), P("dom", "attr"), P("dom", None))
    out_specs = (P("dom", "attr"), P(("dom", "attr"), None))
    return jax.shard_map(shards, mesh=mesh, in_specs=in_specs, out_specs=out_specs, check_vma=False)
```

profile of v0, /device:TPU:0, one launch (start us, length us, event | category | flops | bytes accessed | tf_op | source)
XLA Modules:
  0.0 378.6 jit_solution(3994553369799011512)
XLA Ops:
  7.2 0.0 all-reduce.2.cloned.1.call-start
  7.2 0.7 reduce
  7.9 2.3 reduce-window.6
  10.2 0.3 slice_reduce_fusion
  10.5 0.2 reduce-window.9
  10.7 0.1 add_bitcast_fusion
  10.8 0.7 fusion.8
  11.6 8.0 %scatter_custom_fusion = bf16[3072,256]{1,0:T(8,128)(2,1)S(1)} fusion(s32[1536]{0:T(1024)S(1)} %fusion.8, bf16[1536,256]{1,0:T(8,128)(2,1)} %param.4, bf16[]{:T(256)} %constant.13.clone.1), kind=kCustom, calls=%fused_computation.11 | custom fusion | bytes 1573376 | tf_op jit(solution)/shard_map/scatter | solution.py:27
  19.6 44.1 %all_to_all.34 = bf16[8,384,256]{2,1,0:T(8,128)(2,1)S(1)} all-to-all(bf16[8,384,256]{2,1,0:T(8,128)(2,1)S(1)} %bitcast.34), channel_id=1, replica_groups=mesh['dom'=8,'attr'=4] {'dom'}, dimensions={0} | all-to-all | bytes 3145728 | tf_op jit(solution)/shard_map/all_to_all | solution.py:32
  63.6 4.6 %fusion.12 = f32[3072,512]{1,0:T(8,128)} fusion(bf16[3072,256]{1,0:T(8,128)(2,1)S(1)} %bitcast.31, bf16[512,256]{1,0:T(8,128)(2,1)} %param.6), kind=kOutput, calls=%fused_computation.28 | convolution fusion | flops 805306368 | bytes 8126464 | tf_op jit(solution)/shard_map/dot_general | solution.py:45
  68.3 0.0 all-reduce.2.cloned.1.call-update
  68.3 0.0 reduce-scatter.2.cloned.1.call-start
  68.3 11.1 %scatter_custom_fusion.1 = bf16[3072]{0:T(1024)(128)(2,1)S(1)} fusion(s32[1536]{0:T(1024)S(1)} %fusion.8, bf16[1536]{0:T(1024)(128)(2,1)S(1)} %broadcast.48, bf16[]{:T(256)} %constant.13.clone.1), kind=kCustom, calls=%fused_computation.24 | custom fusion | bytes 6146 | tf_op jit(solution)/shard_map/scatter | solution.py:29
  79.5 0.5 broadcast.58
  80.0 0.7 reduce.6
  80.7 0.1 reshape.84
  80.7 9.9 %all_to_all.35 = bf16[8,2,192]{2,1,0:T(2,128)(2,1)S(1)} all-to-all(bf16[8,2,192]{2,1,0:T(2,128)(2,1)S(1)} %reshape.84), channel_id=1, replica_groups=mesh['dom'=8,'attr'=4] {'dom'}, dimensions={0} | all-to-all | bytes 12288 | tf_op jit(solution)/shard_map/all_to_all | solution.py:39
  90.6 0.1 reshape.85
  90.7 96.3 %all-reduce.2.cloned.1.call-done = f32[3072,512]{1,0:T(8,128)} async-done(((f32[3072,512]{1,0:T(8,128)}), f32[3072,512]{1,0:T(8,128)}) %all-reduce.2.cloned.1.call-update) | async-done | bytes 6291472 | tf_op jit(solution)/shard_map/psum | solution.py:45
  187.0 0.0 copy-start
  187.0 7.5 %fusion.11 = f32[3072]{0:T(1024)S(1)} fusion(s32[3072,512]{1,0:T(8,128)} %param.7, f32[3072,512]{1,0:T(8,128)} %all-reduce.2.cloned.1.call-done), kind=kLoop, calls=%fused_computation.27 | loop fusion | flops 14152704 | bytes 12595200 | tf_op jit(solution)/shard_map/reduce_sum | solution.py:12
  194.6 0.0 copy-done
  194.6 0.0 copy-start.2
  194.6 5.9 %convert_reduce_fusion = (f32[512]{0:T(512)S(1)}, bf16[3072,512]{1,0:T(8,128)(2,1)S(1)}) fusion(f32[3072]{0:T(1024)S(1)} %bitcast.38, f32[3072]{0:T(1024)S(1)} %fusion.11, s32[3072,512]{1,0:T(8,128)} %param.7, f32[3072,512]{1,0:T(8,128)S(1)} %copy-done), kind=kLoop, calls=%fused_computation.2 | loop fusion | flops 20446720 | bytes 15755264 | tf_op jit(solution)/shard_map/reduce_sum | solution.py:48
  200.5 0.0 copy-start.1
  200.5 0.0 copy-done.2
  200.5 2.2 fusion.1
  202.7 0.0 copy-done.1
  202.7 1.7 copy.8
  204.4 22.5 %all_to_all.36 = bf16[4,768,256]{1,2,0:T(8,128)(2,1)S(1)} all-to-all(bf16[4,768,256]{1,2,0:T(8,128)(2,1)S(1)} %copy.8), channel_id=1, replica_groups=mesh['dom'=8,'attr'=4] {'attr'}, dimensions={0} | all-to-all | bytes 3145728 | tf_op jit(solution)/shard_map/all_to_all | solution.py:51
  226.9 3.8 convolution_multiply_fusion
  230.7 0.0 reduce-scatter.2.cloned.1.call-update
  230.7 3.7 fusion.2
  234.4 137.3 %reduce-scatter.2.cloned.1.call-done = f32[32,1024]{1,0:T(8,128)} async-done(((f32[1024,1024]{1,0:T(8,128)}), f32[32,1024]{1,0:T(8,128)}) %reduce-scatter.2.cloned.1.call-update) | async-done | bytes 131088 | tf_op jit(solution)/shard_map/reduce_scatter | solution.py:56
  (7 shorter events, 0.1 us)
Async XLA Ops:
  7.2 179.9 %all-reduce.2.cloned.1.call-start = ((), (), s32[]{:S(2)}) async-start(), calls=%async_computation.4 | async-start | bytes 12582912 | tf_op jit(solution)/shard_map/psum | solution.py:45
  68.3 303.4 %reduce-scatter.2.cloned.1.call-start = ((), (), s32[]{:S(2)}) async-start(), calls=%async_computation.5 | async-start | bytes 4325376 | tf_op jit(solution)/shard_map/reduce_scatter | solution.py:56
  187.0 7.5 %copy-start = (f32[3072,512]{1,0:T(8,128)S(1)}, f32[3072,512]{1,0:T(8,128)}, u32[]{:S(2)}) copy-start(f32[3072,512]{1,0:T(8,128)} %all-reduce.2.cloned.1.call-done) | copy-start | bytes 18874372
  194.6 5.9 %copy-start.2 = (bf16[512,256]{1,0:T(8,128)(2,1)S(1)}, bf16[512,256]{1,0:T(8,128)(2,1)}, u32[]{:S(2)}) copy-start(bf16[512,256]{1,0:T(8,128)(2,1)} %param.6) | copy-start | bytes 786436
  200.5 2.2 copy-start.1
Sparse Core Ops, SparseCore 0:
  68.4 118.5 all-reduce.1
  230.8 140.8 reduce-scatter.1
where the time goes:
time: 379 us
  waiting for transfers between devices  234 us (62%)
  blocking collectives  76.5 us (20%)
  local copies, waits for them, and re-layouts  21.8 us (6%)
  other arithmetic  18.1 us (5%)
  matrix products  14.2 us (4%)
  between operations  14.2 us (4%)
    reduce_scatter x1, waiting for transfers between devices, shards(): lax.psum_scatter(term / total_records, ('dom', 'attr'), scatter_dimension...  137 us
    psum x1, waiting for transfers between devices, shards(): lax.psum(jnp.dot(arrived, entity_means.T, preferred_element_type=jnp.floa...  96.3 us
    all_to_all x1, blocking collectives, shards(): lax.all_to_all(packed.reshape(dom_count, capacity, feat_cols), 'dom', spl...  44.1 us
    all_to_all x1, blocking collectives, shards(): lax.all_to_all(col_resid, 'attr', split_axis=0, concat_axis=1, tiled=True)  22.5 us
    scatter x1, local copies, waits for them, and re-layouts, shards(): jnp.zeros((slot_count,), jnp.bfloat16).at[position]  11.1 us
    all_to_all x1, blocking collectives, shards(): lax.all_to_all(flag_buf.reshape(dom_count, capacity), 'dom', split_axis=0...  9.89 us
    scatter x1, local copies, waits for them, and re-layouts, shards(): jnp.zeros((slot_count, feat_cols), jnp.bfloat16).at[position].set(records)  8.02 us
  transfers between devices with their start and end apart: 2, of which 2 were waited for; matrix products, arithmetic and copies ran while one was open for 4% of the time, Pallas kernels for 0%

commit v1 on v0

--- a/solution.py
+++ b/solution.py
@@ -42,7 +42,12 @@
     )
     arrived = arrived.reshape(slot_count, feat_cols)
     live = arrived_flags.reshape(slot_count).astype(jnp.float32)
-    raw = lax.psum(jnp.dot(arrived, entity_means.T, preferred_element_type=jnp.float32), "attr")
+    raw = jnp.sum(
+        lax.all_gather(
+            jnp.dot(arrived, entity_means.T, preferred_element_type=jnp.float32), "attr"
+        ),
+        axis=0,
+    )
     weights = posterior(raw, noise_bits, live, width)
     sums_cols = jnp.dot(weights.T, arrived, preferred_element_type=jnp.float32)
     mass_col = jnp.sum(weights.astype(jnp.float32), axis=0)[:, None]

time: 379 us -> 428 us (1.13)
  waiting for transfers between devices: 234 us -> 269 us
  other arithmetic: 18.1 us -> 31.5 us
    all_gather x0 -> x1, waiting for transfers between devices: none -> 132 us  [shards(): lax.all_gather(jnp.dot(arrived, entity_means.T, preferred_element_type=jn...]
    psum x1 -> x0, waiting for transfers between devices: 96.3 us -> none  [shards(): lax.psum(jnp.dot(arrived, entity_means.T, preferred_element_type=jnp.floa...]
    reduce_sum x0 -> x1, other arithmetic: none -> 13.1 us  [shards(): jnp.sum(lax.all_gather(jnp.dot(arrived, entity_means.T, preferred_element...]
where the time goes in v1:
time: 428 us; the launch traced here: 427 us
  waiting for transfers between devices  269 us (63%)
  blocking collectives  76.5 us (18%)
  other arithmetic  31.5 us (7%)
  local copies, waits for them, and re-layouts  21.8 us (5%)
  matrix products  14.3 us (3%)
  between operations  14.2 us (3%)
    reduce_scatter x1, waiting for transfers between devices, shards(): lax.psum_scatter(term / total_records, ('dom', 'attr'), scatter_dimension...  138 us
    all_gather x1, waiting for transfers between devices, shards(): lax.all_gather(jnp.dot(arrived, entity_means.T, preferred_element_type=jn...  132 us
    all_to_all x1, blocking collectives, shards(): lax.all_to_all(packed.reshape(dom_count, capacity, feat_cols), 'dom', spl...  44.1 us
    all_to_all x1, blocking collectives, shards(): lax.all_to_all(col_resid, 'attr', split_axis=0, concat_axis=1, tiled=True)  22.5 us
    reduce_sum x1, other arithmetic, shards(): jnp.sum(lax.all_gather(jnp.dot(arrived, entity_means.T, preferred_element...  13.1 us
    scatter x1, local copies, waits for them, and re-layouts, shards(): jnp.zeros((slot_count,), jnp.bfloat16).at[position]  11.1 us
    all_to_all x1, blocking collectives, shards(): lax.all_to_all(flag_buf.reshape(dom_count, capacity), 'dom', split_axis=0...  9.89 us
  transfers between devices with their start and end apart: 2, of which 2 were waited for; matrix products, arithmetic and copies ran while one was open for 4% of the time, Pallas kernels for 0%

profile of v1, /device:TPU:0, one launch (start us, length us, event | category | flops | bytes accessed | tf_op | source)
XLA Modules:
  0.0 427.5 jit_solution(13028503721538253854)
XLA Ops:
  7.2 0.0 all-gather.3.cloned.1.call-start
  7.2 0.7 reduce
  7.9 2.3 reduce-window.6
  10.2 0.3 slice_reduce_fusion
  10.5 0.2 reduce-window.9
  10.7 0.1 add_bitcast_fusion
  10.8 0.7 fusion.8
  11.6 8.0 %scatter_custom_fusion = bf16[3072,256]{1,0:T(8,128)(2,1)S(1)} fusion(s32[1536]{0:T(1024)S(1)} %fusion.8, bf16[1536,256]{1,0:T(8,128)(2,1)} %param.4, bf16[]{:T(256)} %constant.13.clone.1), kind=kCustom, calls=%fused_computation.11 | custom fusion | bytes 1573376 | tf_op jit(solution)/shard_map/scatter | solution.py:27
  19.6 44.1 %all_to_all.34 = bf16[8,384,256]{2,1,0:T(8,128)(2,1)S(1)} all-to-all(bf16[8,384,256]{2,1,0:T(8,128)(2,1)S(1)} %bitcast.36), channel_id=1, replica_groups=mesh['dom'=8,'attr'=4] {'dom'}, dimensions={0} | all-to-all | bytes 3145728 | tf_op jit(solution)/shard_map/all_to_all | solution.py:32
  63.6 4.7 %fusion.12 = f32[3072,512]{1,0:T(8,128)} fusion(bf16[3072,256]{1,0:T(8,128)(2,1)S(1)} %bitcast.33, bf16[512,256]{1,0:T(8,128)(2,1)} %param.6), kind=kOutput, calls=%fused_computation.28 | convolution fusion | flops 805306368 | bytes 8126464 | tf_op jit(solution)/shard_map/dot_general | solution.py:47
  68.3 0.0 all-gather.3.cloned.1.call-update
  68.3 0.0 reduce-scatter.2.cloned.1.call-start
  68.4 11.1 %scatter_custom_fusion.1 = bf16[3072]{0:T(1024)(128)(2,1)S(1)} fusion(s32[1536]{0:T(1024)S(1)} %fusion.8, bf16[1536]{0:T(1024)(128)(2,1)S(1)} %broadcast.48, bf16[]{:T(256)} %constant.13.clone.1), kind=kCustom, calls=%fused_computation.24 | custom fusion | bytes 6146 | tf_op jit(solution)/shard_map/scatter | solution.py:29
  79.5 0.5 broadcast.58
  80.0 0.7 reduce.6
  80.7 0.1 reshape.85
  80.8 9.9 %all_to_all.35 = bf16[8,2,192]{2,1,0:T(2,128)(2,1)S(1)} all-to-all(bf16[8,2,192]{2,1,0:T(2,128)(2,1)S(1)} %reshape.85), channel_id=1, replica_groups=mesh['dom'=8,'attr'=4] {'dom'}, dimensions={0} | all-to-all | bytes 12288 | tf_op jit(solution)/shard_map/all_to_all | solution.py:39
  90.7 0.1 reshape.86
  90.8 131.5 %all-gather.3.cloned.1.call-done = f32[12288,512]{1,0:T(8,128)} async-done(((f32[3072,512]{1,0:T(8,128)}), f32[12288,512]{1,0:T(8,128)}) %all-gather.3.cloned.1.call-update) | async-done | bytes 25165840 | tf_op jit(solution)/shard_map/all_gather | solution.py:46
  222.3 13.1 %reduce_sum.37 = f32[3072,512]{1,0:T(8,128)} reduce(f32[4,3072,512]{2,1,0:T(8,128)} %bitcast.32, f32[]{:T(128)} %constant.8.clone.1), dimensions={0}, to_apply=%region_4.5 | reduce | flops 4718592 | bytes 31457284 | tf_op jit(solution)/shard_map/reduce_sum | solution.py:45
  235.4 0.0 copy-start
  235.4 7.8 %fusion.11 = f32[3072]{0:T(1024)S(1)} fusion(s32[3072,512]{1,0:T(8,128)} %param.7, f32[3072,512]{1,0:T(8,128)} %reduce_sum.37), kind=kLoop, calls=%fused_computation.27 | loop fusion | flops 14152704 | bytes 12595200 | tf_op jit(solution)/shard_map/reduce_sum | solution.py:12
  243.2 0.0 copy-done
  243.2 0.0 copy-start.2
  243.2 5.9 %convert_reduce_fusion = (f32[512]{0:T(512)S(1)}, bf16[3072,512]{1,0:T(8,128)(2,1)S(1)}) fusion(f32[3072]{0:T(1024)S(1)} %bitcast.40, f32[3072]{0:T(1024)S(1)} %fusion.11, s32[3072,512]{1,0:T(8,128)} %param.7, f32[3072,512]{1,0:T(8,128)S(1)} %copy-done), kind=kLoop, calls=%fused_computation.2 | loop fusion | flops 20446720 | bytes 15755264 | tf_op jit(solution)/shard_map/reduce_sum | solution.py:53
  249.1 0.0 copy-start.1
  249.1 0.0 copy-done.2
  249.2 2.2 fusion.1
  251.3 0.0 copy-done.1
  251.3 1.7 copy.8
  253.0 22.5 %all_to_all.36 = bf16[4,768,256]{1,2,0:T(8,128)(2,1)S(1)} all-to-all(bf16[4,768,256]{1,2,0:T(8,128)(2,1)S(1)} %copy.8), channel_id=1, replica_groups=mesh['dom'=8,'attr'=4] {'attr'}, dimensions={0} | all-to-all | bytes 3145728 | tf_op jit(solution)/shard_map/all_to_all | solution.py:56
  275.6 3.7 convolution_multiply_fusion
  279.3 0.0 reduce-scatter.2.cloned.1.call-update
  279.4 3.7 fusion.2
  283.1 137.6 %reduce-scatter.2.cloned.1.call-done = f32[32,1024]{1,0:T(8,128)} async-done(((f32[1024,1024]{1,0:T(8,128)}), f32[32,1024]{1,0:T(8,128)}) %reduce-scatter.2.cloned.1.call-update) | async-done | bytes 131088 | tf_op jit(solution)/shard_map/reduce_scatter | solution.py:61
  (7 shorter events, 0.1 us)
Async XLA Ops:
  7.2 215.2 %all-gather.3.cloned.1.call-start = ((), (), s32[]{:S(2)}) async-start(), calls=%async_computation.5 | async-start | bytes 31457280 | tf_op jit(solution)/shard_map/all_gather | solution.py:46
  68.3 352.3 %reduce-scatter.2.cloned.1.call-start = ((), (), s32[]{:S(2)}) async-start(), calls=%async_computation.4 | async-start | bytes 4325376 | tf_op jit(solution)/shard_map/reduce_scatter | solution.py:61
  235.4 7.8 %copy-start = (f32[3072,512]{1,0:T(8,128)S(1)}, f32[3072,512]{1,0:T(8,128)}, u32[]{:S(2)}) copy-start(f32[3072,512]{1,0:T(8,128)} %reduce_sum.37) | copy-start | bytes 18874372
  243.2 5.9 %copy-start.2 = (bf16[512,256]{1,0:T(8,128)(2,1)S(1)}, bf16[512,256]{1,0:T(8,128)(2,1)}, u32[]{:S(2)}) copy-start(bf16[512,256]{1,0:T(8,128)(2,1)} %param.6) | copy-start | bytes 786436
  249.1 2.2 copy-start.1
Sparse Core Ops, SparseCore 0:
  68.5 153.8 all-gather.2
  279.5 141.1 reduce-scatter.1
